TPU v7x, 32 devices: a whole 2x2x4 slice. The times are simulated.
32 devices in a mesh: comp: 4 (over y, core), tile: 8 (over z, x).
Axes of the slice: x: 2, y: 2, z: 4, core: 2. Of those that a mesh axis runs over, the one named last changes fastest.
Arguments:
- column_state: float32 [4, 8, 4, 16, 2048], P('comp', 'tile'), may hold values from -6 to 6
- mixing: float32 [2, 4, 16], replicated, may hold values from 0.02 to 0.24
- vertical: float32 [2, 16, 16], replicated, may hold values from -1.5 to 1.5
- flux_coef: float32 [2, 4], replicated, may hold values from 0.5 to 1.5
- atm_block: int32 [4, 8, 16], P('comp', 'tile'), may hold values from 0 to 15
- ocean_block: int32 [4, 8, 16], P('comp', 'tile'), may hold values from 0 to 15
- tile_offset: int32 [4, 8, 16], P('comp', 'tile'), may hold values from 0 to 6
- remap_weights: bfloat16 [4, 8, 16, 128, 128], P('comp', 'tile'), may hold values from 0 to 0.119628906
- ocean_mask: int32 [8, 2048], P('tile'), may hold values 0 or 1
Outputs:
- new_state: float32 [4, 8, 4, 16, 2048], P('comp', 'tile')
Inputs may be any that keep to these rules, and one draw needn't show every extreme that they name: `atm_block`: entries at comp index 3 are not read.
All inputs are finite; a program needn't handle non-finite values. No bound on the sum of `ocean_mask` on one device may be relied on, other than what follows from the above.
Results may differ from a plain program's by a relative error of at most 0.0003.
Values sent between devices are 32-bit elements; how exact they have to be, the bound alone decides.
No kernel may reach another device: no remote copies, remote signals or barrier semaphores. Data moves between devices by JAX's collectives and lax.ppermute only.
A program may use at most 64 MiB of HBM per device.

v0:
```python
import jax
import jax.numpy as jnp
from jax import lax
from jax.sharding import PartitionSpec as P

REACH = 3
SUB = 2


def extended(cells, sides, width):
    for axis, dim in sides:
        count = lax.axis_size(axis)
        head = lax.slice_in_dim(cells, 0, width, axis=dim)
        tail = lax.slice_in_dim(cells, cells.shape[dim] - width, cells.shape[dim], axis=dim)
        cells = jnp.concatenate(
            [
                lax.ppermute(tail, axis, [(i, (i + 1) % count) for i in range(count)]),
                cells,
                lax.ppermute(head, axis, [((i + 1) % count, i) for i in range(count)]),
            ],
            axis=dim,
        )
    return cells


def passed_along(value, axis, steps):
    count = lax.axis_size(axis)
    pairs = [(source, (source + steps) % count) for source in range(count)]
    return lax.ppermute(value, axis, pairs)


def local(
    column_state,
    mixing,
    vertical,
    flux_coef,
    atm_block,
    ocean_block,
    tile_offset,
    remap_weights,
    ocean_mask,
):
    fields = column_state[0, 0]
    cells = fields.shape[2]
    across = remap_weights.shape[3]
    ocean_cells = remap_weights.shape[4]
    oblocks = cells // ocean_cells
    spread = 2 * REACH + 1
    comp_index = lax.axis_index("comp")
    comp_count = lax.axis_size("comp")
    is_atmos = comp_index < comp_count - 1
    group = jnp.where(is_atmos, 0, 1).astype(jnp.int32)
    rates = lax.dynamic_index_in_dim(mixing, group, 0, keepdims=False)[:, :, None]
    operator = lax.dynamic_index_in_dim(vertical, group, 0, keepdims=False)
    for sweep in range(SUB):
        padded = extended(fields, (("tile", 2),), 1)
        fields = fields + rates * (padded[:, :, :-2] + padded[:, :, 2:] - 2.0 * fields)
    mixed = fields + jnp.einsum("lm,kmz->klz", operator, fields, precision=lax.Precision.HIGHEST)
    surface = jnp.tanh(flux_coef[0][:, None] * mixed[:, -1] + flux_coef[1][:, None] * mixed[:, -2])
    rounded = surface.astype(jnp.bfloat16)
    blocks = rounded.reshape(rounded.shape[0], cells // across, across)
    chosen = blocks[:, atm_block[0, 0], :]
    contrib = jnp.einsum(
        "knb,nbj->nkj", chosen, remap_weights[0, 0], preferred_element_type=jnp.float32
    )
    by_offset = (tile_offset[0, 0][:, None] == jnp.arange(spread, dtype=jnp.int32)[None, :]).astype(
        jnp.float32
    )
    by_block = (ocean_block[0, 0][:, None] == jnp.arange(oblocks, dtype=jnp.int32)[None, :]).astype(
        jnp.float32
    )
    buffers = jnp.einsum(
        "nd,no,nkj->dkoj", by_offset, by_block, contrib, precision=lax.Precision.HIGHEST
    )
    buffers = buffers.reshape(spread, rounded.shape[0], cells)
    buffers = jnp.where(is_atmos, buffers, 0.0)
    received = buffers[REACH]
    for offset in range(-REACH, REACH + 1):
        if offset != 0:
            received = received + passed_along(buffers[REACH + offset], "tile", offset)
    received = lax.psum(received, "comp")
    land = ocean_mask[0].astype(jnp.float32)
    atmosphere = mixed.at[:, -1].add(-0.5 * surface)
    ocean = mixed.at[:, 0].add(land[None, :] * received)
    result = jnp.where(is_atmos, atmosphere, ocean)
    return result[None, None]


def solution(mesh):
    placed = (
        P("comp", "tile", None, None, None),
        P(),
        P(),
        P(),
        P("comp", "tile", None),
        P("comp", "tile", None),
        P("comp", "tile", None),
        P("comp", "tile", None, None, None),
        P("tile", None),
    )
    return jax.shard_map(
        local,
        mesh=mesh,
        in_specs=placed,
        out_specs=P("comp", "tile", None, None, None),
        check_vma=False,
    )
```

profile of v0, /device:TPU:0, one launch (start us, length us, event | category | flops | bytes accessed | tf_op | source)
XLA Modules:
  0.0 47.1 jit_solution(6400851959491823201)
XLA Ops:
  0.0 0.0 copy-start
  0.0 1.4 %copy.46 = f32[1,1,4,16,2048]{4,2,3,1,0:T(4,128)S(1)} copy(f32[1,1,4,16,2048]{4,3,2,1,0:T(8,128)} %param.13) | data formatting | bytes 1048576 | tf_op args[0]
  1.4 0.1 fusion.36
  1.5 3.0 %collective-permute-start = (f32[4,16,1]{2,0,1:T(4,128)S(1)}, f32[4,16,1]{2,0,1:T(4,128)S(1)}, u32[]{:S(2)}, u32[]{:S(2)}) collective-permute-start(f32[4,16,1]{2,0,1:T(4,128)S(1)} %get-tuple-element.35), channel_id=1, source_target_pairs={{0,1},{1,2},{2,3},{3,4},{4,5},{5,6},{6,7},{7,0},{8,9},{9,10},{10,1... | collective-permute-start | bytes 776 | tf_op jit(solution)/shard_map/ppermute | solution.py:17
  4.5 3.1 %collective-permute-start.1 = (f32[4,16,1]{2,0,1:T(4,128)S(1)}, f32[4,16,1]{2,0,1:T(4,128)S(1)}, u32[]{:S(2)}, u32[]{:S(2)}) collective-permute-start(f32[4,16,1]{2,0,1:T(4,128)S(1)} %get-tuple-element.36), channel_id=1, source_target_pairs={{1,0},{2,1},{3,2},{4,3},{5,4},{6,5},{7,6},{0,7},{9,8},{10,9},{11,1... | collective-permute-start | bytes 776 | tf_op jit(solution)/shard_map/ppermute | solution.py:19
  7.6 0.0 copy-start.4
  7.6 0.7 %copy-done.4 = f32[2,4]{1,0:T(2,128)S(1)} copy-done((f32[2,4]{1,0:T(2,128)S(1)}, f32[2,4]{1,0:T(2,128)}, u32[]{:S(2)}) %copy-start.4) | copy-done | bytes 56
  8.3 0.0 copy-start.7
  8.3 0.6 %copy-done.7 = s32[1,1,16]{2,1,0:T(1,128)S(1)} copy-done((s32[1,1,16]{2,1,0:T(1,128)S(1)}, s32[1,1,16]{2,1,0:T(1,128)}, u32[]{:S(2)}) %copy-start.7) | copy-done | bytes 88
  9.0 0.0 copy-start.5
  9.0 0.7 %copy-done.5 = s32[1,1,16]{2,1,0:T(1,128)S(1)} copy-done((s32[1,1,16]{2,1,0:T(1,128)S(1)}, s32[1,1,16]{2,1,0:T(1,128)}, u32[]{:S(2)}) %copy-start.5) | copy-done | bytes 88
  9.6 0.0 copy-start.6
  9.6 0.7 %copy-done.6 = s32[1,1,16]{2,1,0:T(1,128)S(1)} copy-done((s32[1,1,16]{2,1,0:T(1,128)S(1)}, s32[1,1,16]{2,1,0:T(1,128)}, u32[]{:S(2)}) %copy-start.6) | copy-done | bytes 88
  10.3 0.0 copy-start.3
  10.3 0.7 %copy-done.3 = f32[2,4,16]{2,1,0:T(4,128)S(1)} copy-done((f32[2,4,16]{2,1,0:T(4,128)S(1)}, f32[2,4,16]{2,1,0:T(4,128)}, u32[]{:S(2)}) %copy-start.3) | copy-done | bytes 536
  11.0 0.1 copy.13
  11.1 0.0 collective-permute-done
  11.1 0.0 collective-permute-done.1
  11.1 0.6 %fusion.8 = f32[4,16,2048]{2,0,1:T(4,128)S(1)} fusion(f32[4,16,2048]{2,0,1:T(4,128)S(1)} %bitcast.114, f32[4,16,1]{2,0,1:T(4,128)S(1)} %collective-permute-done.1, f32[4,16,1]{2,0,1:T(4,128)S(1)} %collective-permute-done, f32[4,16]{0,1:T(8,128)S(1)} %copy.13), kind=kLoop, calls=%fused_computation.13 | loop fusion | flops 917504 | bytes 1049344 | tf_op jit(solution)/shard_map/add | solution.py:57
  11.7 0.1 fusion.35
  11.8 0.0 collective-permute-start.2
  11.8 4.7 %collective-permute-start.3 = (f32[4,16,1]{2,0,1:T(4,128)S(1)}, f32[4,16,1]{2,0,1:T(4,128)S(1)}, u32[]{:S(2)}, u32[]{:S(2)}) collective-permute-start(f32[4,16,1]{2,0,1:T(4,128)S(1)} %get-tuple-element.34), channel_id=1, source_target_pairs={{1,0},{2,1},{3,2},{4,3},{5,4},{6,5},{7,6},{0,7},{9,8},{10,9},{11,1... | collective-permute-start | bytes 776 | tf_op jit(solution)/shard_map/ppermute | solution.py:19
  16.5 0.0 copy-start.2
  16.5 1.9 %collective-permute-done.2 = f32[4,16,1]{2,0,1:T(4,128)S(1)} collective-permute-done((f32[4,16,1]{2,0,1:T(4,128)S(1)}, f32[4,16,1]{2,0,1:T(4,128)S(1)}, u32[]{:S(2)}, u32[]{:S(2)}) %collective-permute-start.2) | collective-permute-done | bytes 288 | tf_op jit(solution)/shard_map/ppermute | solution.py:17
  18.4 0.0 collective-permute-done.3
  18.4 0.6 %fusion.4 = f32[4,16,2048]{2,0,1:T(4,128)S(1)} fusion(f32[4,16,2048]{2,0,1:T(4,128)S(1)} %fusion.8, f32[4,16,1]{2,0,1:T(4,128)S(1)} %collective-permute-done.3, f32[4,16,1]{2,0,1:T(4,128)S(1)} %collective-permute-done.2, f32[4,16]{0,1:T(8,128)S(1)} %copy.13), kind=kLoop, calls=%fused_computation.7 | loop fusion | flops 917504 | bytes 1049344 | tf_op jit(solution)/shard_map/add | solution.py:57
  19.1 0.0 copy-done.2
  19.1 0.9 %fusion.11 = f32[4,2048,16]{1,2,0:T(8,128)S(1)} fusion(f32[4,16,2048]{2,0,1:T(4,128)S(1)} %fusion.4, f32[2,16,16]{2,1,0:T(8,128)S(1)} %copy-done.2, s32[]{:T(128)S(6)} %select_n.39), kind=kOutput, calls=%fused_computation.18 | convolution fusion | flops 25165824 | bytes 1056772 | tf_op jit(solution)/shard_map/lm,kmz->klz/dot_general | solution.py:58
  20.0 0.7 %bitcast_add_fusion = f32[4,16,2048]{2,0,1:T(4,128)S(1)} fusion(f32[4,2048,16]{1,2,0:T(8,128)S(1)} %fusion.11, f32[4,16,2048]{2,0,1:T(4,128)S(1)} %fusion.8, f32[4,16,1]{2,0,1:T(4,128)S(1)} %collective-permute-done.3, f32[4,16,1]{2,0,1:T(4,128)S(1)} %collective-permute-done.2, f32[4,16]{0,1:T(8,128)S(1)} %copy.13), kind=kLoop, calls=%fused_computation.17 | loop fusion | flops 1048576 | bytes 1573632 | tf_op jit(solution)/shard_map/add | solution.py:58
  20.7 0.1 fusion.22
  20.8 0.6 %gather_fusion = bf16[16,4,128]{2,1,0:T(4,128)(2,1)S(1)} fusion(bf16[4,16,128]{2,0,1:T(4,128)(2,1)S(1)} %copy.16, s32[1024]{0:T(1024)S(1)} %pad_clamp_fusion), kind=kCustom, calls=%fused_computation | custom fusion | bytes 32832 | tf_op jit(solution)/shard_map/gather | solution.py:62
  21.4 0.0 copy-done
  21.4 0.2 fusion.9
  21.6 0.3 fusion
  22.0 1.6 %collective-permute-start.4 = (f32[4,2048]{1,0:T(4,128)S(1)}, f32[4,2048]{1,0:T(4,128)S(1)}, u32[]{:S(2)}, u32[]{:S(2)}) collective-permute-start(f32[4,2048]{1,0:T(4,128)S(1)} %bitcast.117), channel_id=1, source_target_pairs={{0,5},{1,6},{2,7},{3,0},{4,1},{5,2},{6,3},{7,4},{8,13},{9,14},{10,... | collective-permute-start | bytes 98312 | tf_op jit(solution)/shard_map/ppermute | solution.py:29
  23.7 1.4 %collective-permute-start.5 = (f32[4,2048]{1,0:T(4,128)S(1)}, f32[4,2048]{1,0:T(4,128)S(1)}, u32[]{:S(2)}, u32[]{:S(2)}) collective-permute-start(f32[4,2048]{1,0:T(4,128)S(1)} %bitcast.115), channel_id=1, source_target_pairs={{0,6},{1,7},{2,0},{3,1},{4,2},{5,3},{6,4},{7,5},{8,14},{9,15},{10,... | collective-permute-start | bytes 98312 | tf_op jit(solution)/shard_map/ppermute | solution.py:29
  25.1 1.9 %collective-permute-start.6 = (f32[4,2048]{1,0:T(4,128)S(1)}, f32[4,2048]{1,0:T(4,128)S(1)}, u32[]{:S(2)}, u32[]{:S(2)}) collective-permute-start(f32[4,2048]{1,0:T(4,128)S(1)} %bitcast.116), channel_id=1, source_target_pairs={{0,7},{1,0},{2,1},{3,2},{4,3},{5,4},{6,5},{7,6},{8,15},{9,8},{10,9... | collective-permute-start | bytes 98312 | tf_op jit(solution)/shard_map/ppermute | solution.py:29
  27.0 0.6 %collective-permute-start.7 = (f32[4,2048]{1,0:T(4,128)S(1)}, f32[4,2048]{1,0:T(4,128)S(1)}, u32[]{:S(2)}, u32[]{:S(2)}) collective-permute-start(f32[4,2048]{1,0:T(4,128)S(1)} %bitcast.118), channel_id=1, source_target_pairs={{0,1},{1,2},{2,3},{3,4},{4,5},{5,6},{6,7},{7,0},{8,9},{9,10},{10,1... | collective-permute-start | bytes 98312 | tf_op jit(solution)/shard_map/ppermute | solution.py:29
  27.6 2.1 %collective-permute-start.8 = (f32[4,2048]{1,0:T(4,128)S(1)}, f32[4,2048]{1,0:T(4,128)S(1)}, u32[]{:S(2)}, u32[]{:S(2)}) collective-permute-start(f32[4,2048]{1,0:T(4,128)S(1)} %bitcast.119), channel_id=1, source_target_pairs={{0,2},{1,3},{2,4},{3,5},{4,6},{5,7},{6,0},{7,1},{8,10},{9,11},{10,... | collective-permute-start | bytes 98312 | tf_op jit(solution)/shard_map/ppermute | solution.py:29
  29.6 0.0 copy-start.1
  29.7 0.0 collective-permute-done.4
  29.7 1.5 %collective-permute-start.9 = (f32[4,2048]{1,0:T(4,128)S(1)}, f32[4,2048]{1,0:T(4,128)S(1)}, u32[]{:S(2)}, u32[]{:S(2)}) collective-permute-start(f32[4,2048]{1,0:T(4,128)S(1)} %bitcast.120), channel_id=1, source_target_pairs={{0,3},{1,4},{2,5},{3,6},{4,7},{5,0},{6,1},{7,2},{8,11},{9,12},{10,... | collective-permute-start | bytes 98312 | tf_op jit(solution)/shard_map/ppermute | solution.py:29
  31.2 0.0 copy-done.1
  31.3 0.0 collective-permute-done.5
  31.3 0.0 collective-permute-done.6
  31.3 2.3 %collective-permute-done.7 = f32[4,2048]{1,0:T(4,128)S(1)} collective-permute-done((f32[4,2048]{1,0:T(4,128)S(1)}, f32[4,2048]{1,0:T(4,128)S(1)}, u32[]{:S(2)}, u32[]{:S(2)}) %collective-permute-start.7) | collective-permute-done | bytes 32800 | tf_op jit(solution)/shard_map/ppermute | solution.py:29
  33.6 0.0 collective-permute-done.8
  33.6 1.8 %collective-permute-done.9 = f32[4,2048]{1,0:T(4,128)S(1)} collective-permute-done((f32[4,2048]{1,0:T(4,128)S(1)}, f32[4,2048]{1,0:T(4,128)S(1)}, u32[]{:S(2)}, u32[]{:S(2)}) %collective-permute-start.9) | collective-permute-done | bytes 32800 | tf_op jit(solution)/shard_map/ppermute | solution.py:29
  35.5 10.3 %psum.7 = f32[4,2048]{1,0:T(4,128)S(1)} all-reduce(f32[4,2048]{1,0:T(4,128)S(1)} %fusion.19), channel_id=1, replica_groups=mesh['comp'=4,'tile'=8] {'comp'}, use_global_device_ids=true, to_apply=%region_0.1 | all-reduce | flops 8192 | bytes 65536 | tf_op jit(solution)/shard_map/psum | solution.py:81
  45.8 0.1 add_dynamic-update-slice_fusion
  45.9 0.1 select_bitcast_fusion
  46.0 1.1 %copy.18 = f32[1,1,4,16,2048]{4,3,2,1,0:T(8,128)} copy(f32[1,1,4,16,2048]{4,2,3,1,0:T(4,128)S(1)} %select_bitcast_fusion) | data formatting | bytes 1048576 | tf_op jit(solution)/shard_map/broadcast_in_dim | solution.py:86
  (19 shorter events, 0.3 us)
Async XLA Ops:
  0.0 21.4 %copy-start = (bf16[1,1,16,128,128]{4,3,2,1,0:T(8,128)(2,1)S(1)}, bf16[1,1,16,128,128]{4,3,2,1,0:T(8,128)(2,1)}, u32[]{:S(2)}) copy-start(bf16[1,1,16,128,128]{4,3,2,1,0:T(8,128)(2,1)} %param.20) | copy-start | bytes 1572868
  1.5 9.5 %collective-permute-start = (f32[4,16,1]{2,0,1:T(4,128)S(1)}, f32[4,16,1]{2,0,1:T(4,128)S(1)}, u32[]{:S(2)}, u32[]{:S(2)}) collective-permute-start(f32[4,16,1]{2,0,1:T(4,128)S(1)} %get-tuple-element.35), channel_id=1, source_target_pairs={{0,1},{1,2},{2,3},{3,4},{4,5},{5,6},{6,7},{7,0},{8,9},{9,10},{10,1... | collective-permute-start | bytes 776 | tf_op jit(solution)/shard_map/ppermute | solution.py:17
  4.5 6.5 %collective-permute-start.1 = (f32[4,16,1]{2,0,1:T(4,128)S(1)}, f32[4,16,1]{2,0,1:T(4,128)S(1)}, u32[]{:S(2)}, u32[]{:S(2)}) collective-permute-start(f32[4,16,1]{2,0,1:T(4,128)S(1)} %get-tuple-element.36), channel_id=1, source_target_pairs={{1,0},{2,1},{3,2},{4,3},{5,4},{6,5},{7,6},{0,7},{9,8},{10,9},{11,1... | collective-permute-start | bytes 776 | tf_op jit(solution)/shard_map/ppermute | solution.py:19
  7.6 0.7 %copy-start.4 = (f32[2,4]{1,0:T(2,128)S(1)}, f32[2,4]{1,0:T(2,128)}, u32[]{:S(2)}) copy-start(f32[2,4]{1,0:T(2,128)} %param.16) | copy-start | bytes 100
  8.3 0.7 %copy-start.7 = (s32[1,1,16]{2,1,0:T(1,128)S(1)}, s32[1,1,16]{2,1,0:T(1,128)}, u32[]{:S(2)}) copy-start(s32[1,1,16]{2,1,0:T(1,128)} %param.17) | copy-start | bytes 196
  9.0 0.7 %copy-start.5 = (s32[1,1,16]{2,1,0:T(1,128)S(1)}, s32[1,1,16]{2,1,0:T(1,128)}, u32[]{:S(2)}) copy-start(s32[1,1,16]{2,1,0:T(1,128)} %param.18) | copy-start | bytes 196
  9.6 0.7 %copy-start.6 = (s32[1,1,16]{2,1,0:T(1,128)S(1)}, s32[1,1,16]{2,1,0:T(1,128)}, u32[]{:S(2)}) copy-start(s32[1,1,16]{2,1,0:T(1,128)} %param.19) | copy-start | bytes 196
  10.3 0.7 %copy-start.3 = (f32[2,4,16]{2,1,0:T(4,128)S(1)}, f32[2,4,16]{2,1,0:T(4,128)}, u32[]{:S(2)}) copy-start(f32[2,4,16]{2,1,0:T(4,128)} %param.14) | copy-start | bytes 1540
  11.8 6.6 %collective-permute-start.2 = (f32[4,16,1]{2,0,1:T(4,128)S(1)}, f32[4,16,1]{2,0,1:T(4,128)S(1)}, u32[]{:S(2)}, u32[]{:S(2)}) collective-permute-start(f32[4,16,1]{2,0,1:T(4,128)S(1)} %get-tuple-element.33), channel_id=1, source_target_pairs={{0,1},{1,2},{2,3},{3,4},{4,5},{5,6},{6,7},{7,0},{8,9},{9,10},{10,1... | collective-permute-start | bytes 776 | tf_op jit(solution)/shard_map/ppermute | solution.py:17
  11.8 6.6 %collective-permute-start.3 = (f32[4,16,1]{2,0,1:T(4,128)S(1)}, f32[4,16,1]{2,0,1:T(4,128)S(1)}, u32[]{:S(2)}, u32[]{:S(2)}) collective-permute-start(f32[4,16,1]{2,0,1:T(4,128)S(1)} %get-tuple-element.34), channel_id=1, source_target_pairs={{1,0},{2,1},{3,2},{4,3},{5,4},{6,5},{7,6},{0,7},{9,8},{10,9},{11,1... | collective-permute-start | bytes 776 | tf_op jit(solution)/shard_map/ppermute | solution.py:19
  16.5 2.5 %copy-start.2 = (f32[2,16,16]{2,1,0:T(8,128)S(1)}, f32[2,16,16]{2,1,0:T(8,128)}, u32[]{:S(2)}) copy-start(f32[2,16,16]{2,1,0:T(8,128)} %param.15) | copy-start | bytes 6148
  22.0 7.7 %collective-permute-start.4 = (f32[4,2048]{1,0:T(4,128)S(1)}, f32[4,2048]{1,0:T(4,128)S(1)}, u32[]{:S(2)}, u32[]{:S(2)}) collective-permute-start(f32[4,2048]{1,0:T(4,128)S(1)} %bitcast.117), channel_id=1, source_target_pairs={{0,5},{1,6},{2,7},{3,0},{4,1},{5,2},{6,3},{7,4},{8,13},{9,14},{10,... | collective-permute-start | bytes 98312 | tf_op jit(solution)/shard_map/ppermute | solution.py:29
  23.7 7.6 %collective-permute-start.5 = (f32[4,2048]{1,0:T(4,128)S(1)}, f32[4,2048]{1,0:T(4,128)S(1)}, u32[]{:S(2)}, u32[]{:S(2)}) collective-permute-start(f32[4,2048]{1,0:T(4,128)S(1)} %bitcast.115), channel_id=1, source_target_pairs={{0,6},{1,7},{2,0},{3,1},{4,2},{5,3},{6,4},{7,5},{8,14},{9,15},{10,... | collective-permute-start | bytes 98312 | tf_op jit(solution)/shard_map/ppermute | solution.py:29
  25.1 6.2 %collective-permute-start.6 = (f32[4,2048]{1,0:T(4,128)S(1)}, f32[4,2048]{1,0:T(4,128)S(1)}, u32[]{:S(2)}, u32[]{:S(2)}) collective-permute-start(f32[4,2048]{1,0:T(4,128)S(1)} %bitcast.116), channel_id=1, source_target_pairs={{0,7},{1,0},{2,1},{3,2},{4,3},{5,4},{6,5},{7,6},{8,15},{9,8},{10,9... | collective-permute-start | bytes 98312 | tf_op jit(solution)/shard_map/ppermute | solution.py:29
  27.0 6.7 %collective-permute-start.7 = (f32[4,2048]{1,0:T(4,128)S(1)}, f32[4,2048]{1,0:T(4,128)S(1)}, u32[]{:S(2)}, u32[]{:S(2)}) collective-permute-start(f32[4,2048]{1,0:T(4,128)S(1)} %bitcast.118), channel_id=1, source_target_pairs={{0,1},{1,2},{2,3},{3,4},{4,5},{5,6},{6,7},{7,0},{8,9},{9,10},{10,1... | collective-permute-start | bytes 98312 | tf_op jit(solution)/shard_map/ppermute | solution.py:29
  27.6 6.0 %collective-permute-start.8 = (f32[4,2048]{1,0:T(4,128)S(1)}, f32[4,2048]{1,0:T(4,128)S(1)}, u32[]{:S(2)}, u32[]{:S(2)}) collective-permute-start(f32[4,2048]{1,0:T(4,128)S(1)} %bitcast.119), channel_id=1, source_target_pairs={{0,2},{1,3},{2,4},{3,5},{4,6},{5,7},{6,0},{7,1},{8,10},{9,11},{10,... | collective-permute-start | bytes 98312 | tf_op jit(solution)/shard_map/ppermute | solution.py:29
  29.6 1.5 %copy-start.1 = (s32[1,2048]{1,0:T(1,128)S(1)}, s32[1,2048]{1,0:T(1,128)}, u32[]{:S(2)}) copy-start(s32[1,2048]{1,0:T(1,128)} %param.21) | copy-start | bytes 24580
  29.7 5.8 %collective-permute-start.9 = (f32[4,2048]{1,0:T(4,128)S(1)}, f32[4,2048]{1,0:T(4,128)S(1)}, u32[]{:S(2)}, u32[]{:S(2)}) collective-permute-start(f32[4,2048]{1,0:T(4,128)S(1)} %bitcast.120), channel_id=1, source_target_pairs={{0,3},{1,4},{2,5},{3,6},{4,7},{5,0},{6,1},{7,2},{8,11},{9,12},{10,... | collective-permute-start | bytes 98312 | tf_op jit(solution)/shard_map/ppermute | solution.py:29
where the time goes:
time: 47.4 us; the launch traced here: 47.1 us
  starting transfers between devices  19.9 us (42%)
  blocking collectives  10.3 us (22%)
  local copies, waits for them, and re-layouts  6.88 us (15%)
  waiting for transfers between devices  6.07 us (13%)
  other arithmetic  2.36 us (5%)
  matrix products  1.45 us (3%)
    psum x1, blocking collectives, local(): received = lax.psum(received, 'comp')  10.3 us
    ppermute x6, starting transfers between devices, passed_along(): return lax.ppermute(value, axis, pairs)  9.11 us
    ppermute x2, starting transfers between devices, extended(): lax.ppermute(head, axis, [((i + 1) % count, i) for i in range(count)])  7.81 us
    unnamed x26, local copies, waits for them, and re-layouts  4.92 us
    ppermute x6, waiting for transfers between devices, passed_along(): return lax.ppermute(value, axis, pairs)  4.18 us
    ppermute x2, starting transfers between devices, extended(): lax.ppermute(tail, axis, [(i, (i + 1) % count) for i in range(count)])  3.02 us
    ppermute x2, waiting for transfers between devices, extended(): lax.ppermute(tail, axis, [(i, (i + 1) % count) for i in range(count)])  1.88 us
    add x2, other arithmetic, local(): fields + rates * (padded[:, :, :-2] + padded[:, :, 2:] - 2.0 * fields)  1.28 us
  transfers between devices with their start and end apart: 10, of which 3 were waited for; matrix products, arithmetic and copies ran while one was open for 0% of the time, Pallas kernels for 0%

commit v1 on v0

--- a/solution.py
+++ b/solution.py
@@ -1,10 +1,20 @@
+import functools
 import jax
 import jax.numpy as jnp
 from jax import lax
 from jax.sharding import PartitionSpec as P
+from jax.lax import all_gather
 
 REACH = 3
 SUB = 2
+
+
+def _convert_tails(incoming_x, named_axis):
+    g_now = all_gather(incoming_x, axis_name=named_axis)
+    return jnp.sum(g_now, axis=0)
+
+
+draft_map = functools.partial(_convert_tails, named_axis="comp")
 
 
 def extended(cells, sides, width):
@@ -78,7 +88,7 @@
     for offset in range(-REACH, REACH + 1):
         if offset != 0:
             received = received + passed_along(buffers[REACH + offset], "tile", offset)
-    received = lax.psum(received, "comp")
+    received = draft_map(received)
     land = ocean_mask[0].astype(jnp.float32)
     atmosphere = mixed.at[:, -1].add(-0.5 * surface)
     ocean = mixed.at[:, 0].add(land[None, :] * received)

time: 47.4 us -> 42.6 us (0.90)
  blocking collectives: 10.3 us -> 5.42 us
    psum x1 -> x0, blocking collectives: 10.3 us -> none  [local(): received = lax.psum(received, 'comp')]
    all_gather x0 -> x1, blocking collectives: none -> 5.42 us  [_convert_tails(): g_now = all_gather(incoming_x, axis_name=named_axis)]
  transfers between devices with their start and end apart: 10 -> 10, of which waited for: 3 -> 3; matrix products, arithmetic and copies ran while one was open for 0% -> 1% of each run, Pallas kernels for 0% -> 0%
where the time goes in v1:
time: 42.6 us; the launch traced here: 42.3 us
  starting transfers between devices  19.9 us (47%)
  local copies, waits for them, and re-layouts  6.88 us (16%)
  waiting for transfers between devices  6.07 us (14%)
  blocking collectives  5.42 us (13%)
  other arithmetic  2.38 us (6%)
  matrix products  1.45 us (3%)
    ppermute x6, starting transfers between devices, passed_along(): return lax.ppermute(value, axis, pairs)  9.11 us
    ppermute x2, starting transfers between devices, extended(): lax.ppermute(head, axis, [((i + 1) % count, i) for i in range(count)])  7.81 us
    all_gather x1, blocking collectives, _convert_tails(): g_now = all_gather(incoming_x, axis_name=named_axis)  5.42 us
    unnamed x26, local copies, waits for them, and re-layouts  4.92 us
    ppermute x6, waiting for transfers between devices, passed_along(): return lax.ppermute(value, axis, pairs)  4.18 us
    ppermute x2, starting transfers between devices, extended(): lax.ppermute(tail, axis, [(i, (i + 1) % count) for i in range(count)])  3.02 us
    ppermute x2, waiting for transfers between devices, extended(): lax.ppermute(tail, axis, [(i, (i + 1) % count) for i in range(count)])  1.88 us
    add x2, other arithmetic, local(): fields + rates * (padded[:, :, :-2] + padded[:, :, 2:] - 2.0 * fields)  1.28 us
  transfers between devices with their start and end apart: 10, of which 3 were waited for; matrix products, arithmetic and copies ran while one was open for 1% of the time, Pallas kernels for 0%

profile of v1, /device:TPU:0, one launch (start us, length us, event | category | flops | bytes accessed | tf_op | source)
XLA Modules:
  0.0 42.3 jit_solution(9136632991708031139)
XLA Ops:
  0.0 0.0 copy-start
  0.0 1.4 %copy.49 = f32[1,1,4,16,2048]{4,2,3,1,0:T(4,128)S(1)} copy(f32[1,1,4,16,2048]{4,3,2,1,0:T(8,128)} %param.13) | data formatting | bytes 1048576 | tf_op args[0]
  1.4 0.1 fusion.37
  1.5 3.0 %collective-permute-start = (f32[4,16,1]{2,0,1:T(4,128)S(1)}, f32[4,16,1]{2,0,1:T(4,128)S(1)}, u32[]{:S(2)}, u32[]{:S(2)}) collective-permute-start(f32[4,16,1]{2,0,1:T(4,128)S(1)} %get-tuple-element.35), channel_id=1, source_target_pairs={{0,1},{1,2},{2,3},{3,4},{4,5},{5,6},{6,7},{7,0},{8,9},{9,10},{10,1... | collective-permute-start | bytes 776 | tf_op jit(solution)/shard_map/ppermute | solution.py:27
  4.5 3.1 %collective-permute-start.1 = (f32[4,16,1]{2,0,1:T(4,128)S(1)}, f32[4,16,1]{2,0,1:T(4,128)S(1)}, u32[]{:S(2)}, u32[]{:S(2)}) collective-permute-start(f32[4,16,1]{2,0,1:T(4,128)S(1)} %get-tuple-element.36), channel_id=1, source_target_pairs={{1,0},{2,1},{3,2},{4,3},{5,4},{6,5},{7,6},{0,7},{9,8},{10,9},{11,1... | collective-permute-start | bytes 776 | tf_op jit(solution)/shard_map/ppermute | solution.py:29
  7.6 0.0 copy-start.4
  7.6 0.7 %copy-done.4 = f32[2,4]{1,0:T(2,128)S(1)} copy-done((f32[2,4]{1,0:T(2,128)S(1)}, f32[2,4]{1,0:T(2,128)}, u32[]{:S(2)}) %copy-start.4) | copy-done | bytes 56
  8.3 0.0 copy-start.7
  8.3 0.6 %copy-done.7 = s32[1,1,16]{2,1,0:T(1,128)S(1)} copy-done((s32[1,1,16]{2,1,0:T(1,128)S(1)}, s32[1,1,16]{2,1,0:T(1,128)}, u32[]{:S(2)}) %copy-start.7) | copy-done | bytes 88
  9.0 0.0 copy-start.5
  9.0 0.7 %copy-done.5 = s32[1,1,16]{2,1,0:T(1,128)S(1)} copy-done((s32[1,1,16]{2,1,0:T(1,128)S(1)}, s32[1,1,16]{2,1,0:T(1,128)}, u32[]{:S(2)}) %copy-start.5) | copy-done | bytes 88
  9.6 0.0 copy-start.6
  9.6 0.7 %copy-done.6 = s32[1,1,16]{2,1,0:T(1,128)S(1)} copy-done((s32[1,1,16]{2,1,0:T(1,128)S(1)}, s32[1,1,16]{2,1,0:T(1,128)}, u32[]{:S(2)}) %copy-start.6) | copy-done | bytes 88
  10.3 0.0 copy-start.3
  10.3 0.7 %copy-done.3 = f32[2,4,16]{2,1,0:T(4,128)S(1)} copy-done((f32[2,4,16]{2,1,0:T(4,128)S(1)}, f32[2,4,16]{2,1,0:T(4,128)}, u32[]{:S(2)}) %copy-start.3) | copy-done | bytes 536
  11.0 0.1 copy.16
  11.1 0.0 collective-permute-done
  11.1 0.0 collective-permute-done.1
  11.1 0.6 %fusion.8 = f32[4,16,2048]{2,0,1:T(4,128)S(1)} fusion(f32[4,16,2048]{2,0,1:T(4,128)S(1)} %bitcast.120, f32[4,16,1]{2,0,1:T(4,128)S(1)} %collective-permute-done.1, f32[4,16,1]{2,0,1:T(4,128)S(1)} %collective-permute-done, f32[4,16]{0,1:T(8,128)S(1)} %copy.16), kind=kLoop, calls=%fused_computation.13 | loop fusion | flops 917504 | bytes 1049344 | tf_op jit(solution)/shard_map/add | solution.py:67
  11.7 0.1 fusion.36
  11.8 0.0 collective-permute-start.2
  11.8 4.7 %collective-permute-start.3 = (f32[4,16,1]{2,0,1:T(4,128)S(1)}, f32[4,16,1]{2,0,1:T(4,128)S(1)}, u32[]{:S(2)}, u32[]{:S(2)}) collective-permute-start(f32[4,16,1]{2,0,1:T(4,128)S(1)} %get-tuple-element.34), channel_id=1, source_target_pairs={{1,0},{2,1},{3,2},{4,3},{5,4},{6,5},{7,6},{0,7},{9,8},{10,9},{11,1... | collective-permute-start | bytes 776 | tf_op jit(solution)/shard_map/ppermute | solution.py:29
  16.5 0.0 copy-start.2
  16.5 1.9 %collective-permute-done.2 = f32[4,16,1]{2,0,1:T(4,128)S(1)} collective-permute-done((f32[4,16,1]{2,0,1:T(4,128)S(1)}, f32[4,16,1]{2,0,1:T(4,128)S(1)}, u32[]{:S(2)}, u32[]{:S(2)}) %collective-permute-start.2) | collective-permute-done | bytes 288 | tf_op jit(solution)/shard_map/ppermute | solution.py:27
  18.4 0.0 collective-permute-done.3
  18.4 0.6 %fusion.4 = f32[4,16,2048]{2,0,1:T(4,128)S(1)} fusion(f32[4,16,2048]{2,0,1:T(4,128)S(1)} %fusion.8, f32[4,16,1]{2,0,1:T(4,128)S(1)} %collective-permute-done.3, f32[4,16,1]{2,0,1:T(4,128)S(1)} %collective-permute-done.2, f32[4,16]{0,1:T(8,128)S(1)} %copy.16), kind=kLoop, calls=%fused_computation.7 | loop fusion | flops 917504 | bytes 1049344 | tf_op jit(solution)/shard_map/add | solution.py:67
  19.1 0.0 copy-done.2
  19.1 0.9 %fusion.11 = f32[4,2048,16]{1,2,0:T(8,128)S(1)} fusion(f32[4,16,2048]{2,0,1:T(4,128)S(1)} %fusion.4, f32[2,16,16]{2,1,0:T(8,128)S(1)} %copy-done.2, s32[]{:T(128)S(6)} %select_n.39), kind=kOutput, calls=%fused_computation.18 | convolution fusion | flops 25165824 | bytes 1056772 | tf_op jit(solution)/shard_map/lm,kmz->klz/dot_general | solution.py:68
  20.0 0.7 %bitcast_add_fusion = f32[4,16,2048]{2,0,1:T(4,128)S(1)} fusion(f32[4,2048,16]{1,2,0:T(8,128)S(1)} %fusion.11, f32[4,16,2048]{2,0,1:T(4,128)S(1)} %fusion.8, f32[4,16,1]{2,0,1:T(4,128)S(1)} %collective-permute-done.3, f32[4,16,1]{2,0,1:T(4,128)S(1)} %collective-permute-done.2, f32[4,16]{0,1:T(8,128)S(1)} %copy.16), kind=kLoop, calls=%fused_computation.17 | loop fusion | flops 1048576 | bytes 1573632 | tf_op jit(solution)/shard_map/add | solution.py:68
  20.7 0.1 fusion.23
  20.8 0.6 %gather_fusion = bf16[16,4,128]{2,1,0:T(4,128)(2,1)S(1)} fusion(bf16[4,16,128]{2,0,1:T(4,128)(2,1)S(1)} %copy.19, s32[1024]{0:T(1024)S(1)} %pad_clamp_fusion), kind=kCustom, calls=%fused_computation | custom fusion | bytes 32832 | tf_op jit(solution)/shard_map/gather | solution.py:72
  21.4 0.0 copy-done
  21.4 0.2 fusion.9
  21.6 0.3 fusion
  22.0 1.6 %collective-permute-start.4 = (f32[4,2048]{1,0:T(4,128)S(1)}, f32[4,2048]{1,0:T(4,128)S(1)}, u32[]{:S(2)}, u32[]{:S(2)}) collective-permute-start(f32[4,2048]{1,0:T(4,128)S(1)} %bitcast.123), channel_id=1, source_target_pairs={{0,5},{1,6},{2,7},{3,0},{4,1},{5,2},{6,3},{7,4},{8,13},{9,14},{10,... | collective-permute-start | bytes 98312 | tf_op jit(solution)/shard_map/ppermute | solution.py:39
  23.7 1.4 %collective-permute-start.5 = (f32[4,2048]{1,0:T(4,128)S(1)}, f32[4,2048]{1,0:T(4,128)S(1)}, u32[]{:S(2)}, u32[]{:S(2)}) collective-permute-start(f32[4,2048]{1,0:T(4,128)S(1)} %bitcast.121), channel_id=1, source_target_pairs={{0,6},{1,7},{2,0},{3,1},{4,2},{5,3},{6,4},{7,5},{8,14},{9,15},{10,... | collective-permute-start | bytes 98312 | tf_op jit(solution)/shard_map/ppermute | solution.py:39
  25.1 1.9 %collective-permute-start.6 = (f32[4,2048]{1,0:T(4,128)S(1)}, f32[4,2048]{1,0:T(4,128)S(1)}, u32[]{:S(2)}, u32[]{:S(2)}) collective-permute-start(f32[4,2048]{1,0:T(4,128)S(1)} %bitcast.122), channel_id=1, source_target_pairs={{0,7},{1,0},{2,1},{3,2},{4,3},{5,4},{6,5},{7,6},{8,15},{9,8},{10,9... | collective-permute-start | bytes 98312 | tf_op jit(solution)/shard_map/ppermute | solution.py:39
  27.0 0.6 %collective-permute-start.7 = (f32[4,2048]{1,0:T(4,128)S(1)}, f32[4,2048]{1,0:T(4,128)S(1)}, u32[]{:S(2)}, u32[]{:S(2)}) collective-permute-start(f32[4,2048]{1,0:T(4,128)S(1)} %bitcast.124), channel_id=1, source_target_pairs={{0,1},{1,2},{2,3},{3,4},{4,5},{5,6},{6,7},{7,0},{8,9},{9,10},{10,1... | collective-permute-start | bytes 98312 | tf_op jit(solution)/shard_map/ppermute | solution.py:39
  27.6 2.1 %collective-permute-start.8 = (f32[4,2048]{1,0:T(4,128)S(1)}, f32[4,2048]{1,0:T(4,128)S(1)}, u32[]{:S(2)}, u32[]{:S(2)}) collective-permute-start(f32[4,2048]{1,0:T(4,128)S(1)} %bitcast.125), channel_id=1, source_target_pairs={{0,2},{1,3},{2,4},{3,5},{4,6},{5,7},{6,0},{7,1},{8,10},{9,11},{10,... | collective-permute-start | bytes 98312 | tf_op jit(solution)/shard_map/ppermute | solution.py:39
  29.6 0.0 copy-start.1
  29.7 0.0 collective-permute-done.4
  29.7 1.5 %collective-permute-start.9 = (f32[4,2048]{1,0:T(4,128)S(1)}, f32[4,2048]{1,0:T(4,128)S(1)}, u32[]{:S(2)}, u32[]{:S(2)}) collective-permute-start(f32[4,2048]{1,0:T(4,128)S(1)} %bitcast.126), channel_id=1, source_target_pairs={{0,3},{1,4},{2,5},{3,6},{4,7},{5,0},{6,1},{7,2},{8,11},{9,12},{10,... | collective-permute-start | bytes 98312 | tf_op jit(solution)/shard_map/ppermute | solution.py:39
  31.2 0.0 copy-done.1
  31.3 0.0 collective-permute-done.5
  31.3 0.0 collective-permute-done.6
  31.3 2.3 %collective-permute-done.7 = f32[4,2048]{1,0:T(4,128)S(1)} collective-permute-done((f32[4,2048]{1,0:T(4,128)S(1)}, f32[4,2048]{1,0:T(4,128)S(1)}, u32[]{:S(2)}, u32[]{:S(2)}) %collective-permute-start.7) | collective-permute-done | bytes 32800 | tf_op jit(solution)/shard_map/ppermute | solution.py:39
  33.6 0.0 collective-permute-done.8
  33.6 1.8 %collective-permute-done.9 = f32[4,2048]{1,0:T(4,128)S(1)} collective-permute-done((f32[4,2048]{1,0:T(4,128)S(1)}, f32[4,2048]{1,0:T(4,128)S(1)}, u32[]{:S(2)}, u32[]{:S(2)}) %collective-permute-start.9) | collective-permute-done | bytes 32800 | tf_op jit(solution)/shard_map/ppermute | solution.py:39
  35.5 5.4 %all-gather.1 = f32[4,4,2048]{2,1,0:T(4,128)S(1)} all-gather(f32[1,4,2048]{2,1,0:T(4,128)S(1)} %fusion.20), channel_id=2, replica_groups=mesh['comp'=4,'tile'=8] {'comp'}, dimensions={0}, use_global_device_ids=true | all-gather | bytes 163840 | tf_op jit(solution)/shard_map/all_gather | solution.py:13
  41.0 0.1 add_dynamic-update-slice_fusion
  41.1 0.1 select_bitcast_fusion
  41.2 1.1 %copy.21 = f32[1,1,4,16,2048]{4,3,2,1,0:T(8,128)} copy(f32[1,1,4,16,2048]{4,2,3,1,0:T(4,128)S(1)} %select_bitcast_fusion) | data formatting | bytes 1048576 | tf_op jit(solution)/shard_map/broadcast_in_dim | solution.py:96
  (20 shorter events, 0.3 us)
Async XLA Ops:
  0.0 21.4 %copy-start = (bf16[1,1,16,128,128]{4,3,2,1,0:T(8,128)(2,1)S(1)}, bf16[1,1,16,128,128]{4,3,2,1,0:T(8,128)(2,1)}, u32[]{:S(2)}) copy-start(bf16[1,1,16,128,128]{4,3,2,1,0:T(8,128)(2,1)} %param.20) | copy-start | bytes 1572868
  1.5 9.5 %collective-permute-start = (f32[4,16,1]{2,0,1:T(4,128)S(1)}, f32[4,16,1]{2,0,1:T(4,128)S(1)}, u32[]{:S(2)}, u32[]{:S(2)}) collective-permute-start(f32[4,16,1]{2,0,1:T(4,128)S(1)} %get-tuple-element.35), channel_id=1, source_target_pairs={{0,1},{1,2},{2,3},{3,4},{4,5},{5,6},{6,7},{7,0},{8,9},{9,10},{10,1... | collective-permute-start | bytes 776 | tf_op jit(solution)/shard_map/ppermute | solution.py:27
  4.5 6.5 %collective-permute-start.1 = (f32[4,16,1]{2,0,1:T(4,128)S(1)}, f32[4,16,1]{2,0,1:T(4,128)S(1)}, u32[]{:S(2)}, u32[]{:S(2)}) collective-permute-start(f32[4,16,1]{2,0,1:T(4,128)S(1)} %get-tuple-element.36), channel_id=1, source_target_pairs={{1,0},{2,1},{3,2},{4,3},{5,4},{6,5},{7,6},{0,7},{9,8},{10,9},{11,1... | collective-permute-start | bytes 776 | tf_op jit(solution)/shard_map/ppermute | solution.py:29
  7.6 0.7 %copy-start.4 = (f32[2,4]{1,0:T(2,128)S(1)}, f32[2,4]{1,0:T(2,128)}, u32[]{:S(2)}) copy-start(f32[2,4]{1,0:T(2,128)} %param.16) | copy-start | bytes 100
  8.3 0.7 %copy-start.7 = (s32[1,1,16]{2,1,0:T(1,128)S(1)}, s32[1,1,16]{2,1,0:T(1,128)}, u32[]{:S(2)}) copy-start(s32[1,1,16]{2,1,0:T(1,128)} %param.17) | copy-start | bytes 196
  9.0 0.7 %copy-start.5 = (s32[1,1,16]{2,1,0:T(1,128)S(1)}, s32[1,1,16]{2,1,0:T(1,128)}, u32[]{:S(2)}) copy-start(s32[1,1,16]{2,1,0:T(1,128)} %param.18) | copy-start | bytes 196
  9.6 0.7 %copy-start.6 = (s32[1,1,16]{2,1,0:T(1,128)S(1)}, s32[1,1,16]{2,1,0:T(1,128)}, u32[]{:S(2)}) copy-start(s32[1,1,16]{2,1,0:T(1,128)} %param.19) | copy-start | bytes 196
  10.3 0.7 %copy-start.3 = (f32[2,4,16]{2,1,0:T(4,128)S(1)}, f32[2,4,16]{2,1,0:T(4,128)}, u32[]{:S(2)}) copy-start(f32[2,4,16]{2,1,0:T(4,128)} %param.14) | copy-start | bytes 1540
  11.8 6.6 %collective-permute-start.2 = (f32[4,16,1]{2,0,1:T(4,128)S(1)}, f32[4,16,1]{2,0,1:T(4,128)S(1)}, u32[]{:S(2)}, u32[]{:S(2)}) collective-permute-start(f32[4,16,1]{2,0,1:T(4,128)S(1)} %get-tuple-element.33), channel_id=1, source_target_pairs={{0,1},{1,2},{2,3},{3,4},{4,5},{5,6},{6,7},{7,0},{8,9},{9,10},{10,1... | collective-permute-start | bytes 776 | tf_op jit(solution)/shard_map/ppermute | solution.py:27
  11.8 6.6 %collective-permute-start.3 = (f32[4,16,1]{2,0,1:T(4,128)S(1)}, f32[4,16,1]{2,0,1:T(4,128)S(1)}, u32[]{:S(2)}, u32[]{:S(2)}) collective-permute-start(f32[4,16,1]{2,0,1:T(4,128)S(1)} %get-tuple-element.34), channel_id=1, source_target_pairs={{1,0},{2,1},{3,2},{4,3},{5,4},{6,5},{7,6},{0,7},{9,8},{10,9},{11,1... | collective-permute-start | bytes 776 | tf_op jit(solution)/shard_map/ppermute | solution.py:29
  16.5 2.5 %copy-start.2 = (f32[2,16,16]{2,1,0:T(8,128)S(1)}, f32[2,16,16]{2,1,0:T(8,128)}, u32[]{:S(2)}) copy-start(f32[2,16,16]{2,1,0:T(8,128)} %param.15) | copy-start | bytes 6148
  22.0 7.7 %collective-permute-start.4 = (f32[4,2048]{1,0:T(4,128)S(1)}, f32[4,2048]{1,0:T(4,128)S(1)}, u32[]{:S(2)}, u32[]{:S(2)}) collective-permute-start(f32[4,2048]{1,0:T(4,128)S(1)} %bitcast.123), channel_id=1, source_target_pairs={{0,5},{1,6},{2,7},{3,0},{4,1},{5,2},{6,3},{7,4},{8,13},{9,14},{10,... | collective-permute-start | bytes 98312 | tf_op jit(solution)/shard_map/ppermute | solution.py:39
  23.7 7.6 %collective-permute-start.5 = (f32[4,2048]{1,0:T(4,128)S(1)}, f32[4,2048]{1,0:T(4,128)S(1)}, u32[]{:S(2)}, u32[]{:S(2)}) collective-permute-start(f32[4,2048]{1,0:T(4,128)S(1)} %bitcast.121), channel_id=1, source_target_pairs={{0,6},{1,7},{2,0},{3,1},{4,2},{5,3},{6,4},{7,5},{8,14},{9,15},{10,... | collective-permute-start | bytes 98312 | tf_op jit(solution)/shard_map/ppermute | solution.py:39
  25.1 6.2 %collective-permute-start.6 = (f32[4,2048]{1,0:T(4,128)S(1)}, f32[4,2048]{1,0:T(4,128)S(1)}, u32[]{:S(2)}, u32[]{:S(2)}) collective-permute-start(f32[4,2048]{1,0:T(4,128)S(1)} %bitcast.122), channel_id=1, source_target_pairs={{0,7},{1,0},{2,1},{3,2},{4,3},{5,4},{6,5},{7,6},{8,15},{9,8},{10,9... | collective-permute-start | bytes 98312 | tf_op jit(solution)/shard_map/ppermute | solution.py:39
  27.0 6.7 %collective-permute-start.7 = (f32[4,2048]{1,0:T(4,128)S(1)}, f32[4,2048]{1,0:T(4,128)S(1)}, u32[]{:S(2)}, u32[]{:S(2)}) collective-permute-start(f32[4,2048]{1,0:T(4,128)S(1)} %bitcast.124), channel_id=1, source_target_pairs={{0,1},{1,2},{2,3},{3,4},{4,5},{5,6},{6,7},{7,0},{8,9},{9,10},{10,1... | collective-permute-start | bytes 98312 | tf_op jit(solution)/shard_map/ppermute | solution.py:39
  27.6 6.0 %collective-permute-start.8 = (f32[4,2048]{1,0:T(4,128)S(1)}, f32[4,2048]{1,0:T(4,128)S(1)}, u32[]{:S(2)}, u32[]{:S(2)}) collective-permute-start(f32[4,2048]{1,0:T(4,128)S(1)} %bitcast.125), channel_id=1, source_target_pairs={{0,2},{1,3},{2,4},{3,5},{4,6},{5,7},{6,0},{7,1},{8,10},{9,11},{10,... | collective-permute-start | bytes 98312 | tf_op jit(solution)/shard_map/ppermute | solution.py:39
  29.6 1.5 %copy-start.1 = (s32[1,2048]{1,0:T(1,128)S(1)}, s32[1,2048]{1,0:T(1,128)}, u32[]{:S(2)}) copy-start(s32[1,2048]{1,0:T(1,128)} %param.21) | copy-start | bytes 24580
  29.7 5.8 %collective-permute-start.9 = (f32[4,2048]{1,0:T(4,128)S(1)}, f32[4,2048]{1,0:T(4,128)S(1)}, u32[]{:S(2)}, u32[]{:S(2)}) collective-permute-start(f32[4,2048]{1,0:T(4,128)S(1)} %bitcast.126), channel_id=1, source_target_pairs={{0,3},{1,4},{2,5},{3,6},{4,7},{5,0},{6,1},{7,2},{8,11},{9,12},{10,... | collective-permute-start | bytes 98312 | tf_op jit(solution)/shard_map/ppermute | solution.py:39
